TPU v7x, 32 devices: a whole 2x2x4 slice. The times are simulated.
32 devices in a mesh: dp: 8 (over z, y), tensor: 4 (over x, core).
Axes of the slice: x: 2, y: 2, z: 4, core: 2. Of those that a mesh axis runs over, the one named last changes fastest.
Arguments:
- inputs: bfloat16 [16, 1024, 768], P('dp', 'tensor'), may hold values from -6 to 6
- segment_ids: int32 [16, 1024], P('dp'), may hold values from 0 to 11, never falling along the last dimension, each value on 1 to 512 neighbouring positions
- cotangent: bfloat16 [16, 1024, 768], P('dp', 'tensor'), may hold values from -6 to 6
- w_query: bfloat16 [768, 768], P(None, 'tensor'), may hold values from -0.21875 to 0.21875
- w_key: bfloat16 [768, 768], P(None, 'tensor'), may hold values from -0.21875 to 0.21875
- w_value: bfloat16 [768, 768], P(None, 'tensor'), may hold values from -0.21875 to 0.21875
- b_query: float32 [768], P('tensor'), may hold values from -3 to 3
- b_value: float32 [768], P('tensor'), may hold values from -3 to 3
- w_out: bfloat16 [768, 768], P('tensor'), may hold values from -1.25 to 1.25
- b_out: float32 [768], replicated, may hold values from -2 to 2
- gain_one: float32 [768], replicated, may hold values from 0.5 to 1.5
- shift_one: float32 [768], replicated, may hold values from -2 to 2
- w_up: bfloat16 [768, 3072], P(None, 'tensor'), may hold values from -0.21875 to 0.21875
- b_up: float32 [3072], P('tensor'), may hold values from -3 to 3
- w_down: bfloat16 [3072, 768], P('tensor'), may hold values from -0.109375 to 0.109375
- b_down: float32 [768], replicated, may hold values from -2 to 2
- gain_two: float32 [768], replicated, may hold values from 0.5 to 1.5
- shift_two: float32 [768], replicated, may hold values from -2 to 2
Outputs:
- output: bfloat16 [16, 1024, 768], P('dp', 'tensor')
- grad_input: float32 [16, 1024, 768], P('dp', 'tensor')
- grad_w_query: float32 [768, 768], P(None, 'tensor')
- grad_w_key: float32 [768, 768], P(None, 'tensor')
- grad_w_value: float32 [768, 768], P(None, 'tensor')
- grad_b_query: float32 [768], P('tensor')
- grad_b_value: float32 [768], P('tensor')
- grad_w_out: float32 [768, 768], P('tensor')
- grad_b_out: float32 [768], replicated
- grad_gain_one: float32 [768], replicated
- grad_shift_one: float32 [768], replicated
- grad_w_up: float32 [768, 3072], P(None, 'tensor')
- grad_b_up: float32 [3072], P('tensor')
- grad_w_down: float32 [3072, 768], P('tensor')
- grad_b_down: float32 [768], replicated
- grad_gain_two: float32 [768], replicated
- grad_shift_two: float32 [768], replicated
Inputs may be any that keep to these rules, and one draw needn't show every extreme that they name: `segment_ids`: along each sequence the ids never fall; each of the 12 documents of a sequence holds 1 to 512 consecutive tokens, and some document has exactly 512 of them.
All inputs are finite; a program needn't handle non-finite values.
Results may differ from a plain program's by a relative error of at most 0.018.
Values may be sent and summed in bfloat16 or wider, within the bound.
No kernel may reach another device: no remote copies, remote signals or barrier semaphores. Data moves between devices by JAX's collectives and lax.ppermute only.
A program may use at most 128 MiB of HBM per device.

v0:
```python
from functools import partial
import math

import jax
import jax.numpy as jnp
from jax import lax
from jax.sharding import PartitionSpec as P

HEAD_DIM = 64


LAYER_EPSILON = 1e-05


def layer_norm(rows, gain, shift):
    average = jnp.mean(rows, -1, keepdims=True)
    centred = rows - average
    variance = jnp.mean(centred * centred, -1, keepdims=True)
    return centred * lax.rsqrt(variance + LAYER_EPSILON) * gain + shift


def matmul(left, right):
    return jnp.dot(left, right, preferred_element_type=jnp.float32)


def add_tuple(running, addition):
    return tuple((first_term + second_term for first_term, second_term in zip(running, addition)))


def shards(
    inputs,
    segment_ids,
    cotangent,
    w_query,
    w_key,
    w_value,
    b_query,
    b_value,
    w_out,
    b_out,
    gain_one,
    shift_one,
    w_up,
    b_up,
    w_down,
    b_down,
    gain_two,
    shift_two,
):
    local_rows = inputs.shape[1]
    length = local_rows * lax.axis_size("tensor")
    local_width = w_query.shape[1]
    local_heads = local_width // HEAD_DIM
    score_scale = 1.0 / math.sqrt(HEAD_DIM)
    block_rows = min(512, length)
    block_total = length // block_rows
    split_params = (w_query, w_key, w_value, b_query, b_value, w_out, w_up, b_up, w_down)
    shared_params = (b_out, gain_one, shift_one, b_down, gain_two, shift_two)

    def micro_pass(input_rows, segment_row, cotangent_rows):
        inputs_full = lax.all_gather(input_rows, "tensor", axis=0, tiled=True)
        query = (matmul(inputs_full, w_query) + b_query).astype(jnp.bfloat16)
        keys = matmul(inputs_full, w_key).astype(jnp.bfloat16)
        values = (matmul(inputs_full, w_value) + b_value).astype(jnp.bfloat16)
        query_heads = query.reshape(length, local_heads, HEAD_DIM)
        key_heads = keys.reshape(length, local_heads, HEAD_DIM)
        value_heads = values.reshape(length, local_heads, HEAD_DIM)

        def block_scores(first_row):
            query_block = query_heads[first_row : first_row + block_rows]
            scaled = (
                jnp.einsum(
                    "qhd,khd->hqk", query_block, key_heads, preferred_element_type=jnp.float32
                )
                * score_scale
            )
            same_doc = segment_row[first_row : first_row + block_rows, None] == segment_row[None, :]
            return (jnp.where(same_doc[None], scaled, -1e30), query_block)

        context_parts = []
        logsum_parts = []
        for block_index in range(block_total):
            masked, query_block = block_scores(block_index * block_rows)
            row_max = jnp.max(masked, -1, keepdims=True)
            exponent = jnp.exp(masked - row_max)
            row_sum = jnp.sum(exponent, -1, keepdims=True)
            attention = (exponent / row_sum).astype(jnp.bfloat16)
            context_parts.append(
                jnp.einsum(
                    "hqk,khd->qhd", attention, value_heads, preferred_element_type=jnp.float32
                )
            )
            logsum_parts.append(row_max + jnp.log(row_sum))
        context = (
            jnp.concatenate(context_parts, 0).reshape(length, local_width).astype(jnp.bfloat16)
        )
        log_sums = jnp.concatenate(logsum_parts, 1)
        attended = (
            lax.psum_scatter(matmul(context, w_out), "tensor", scatter_dimension=0, tiled=True)
            + b_out
        )
        residual_one = input_rows.astype(jnp.float32) + attended
        hidden_one, norm_one_back = jax.vjp(layer_norm, residual_one, gain_one, shift_one)
        hidden_full = lax.all_gather(hidden_one.astype(jnp.bfloat16), "tensor", axis=0, tiled=True)
        before_gelu = matmul(hidden_full, w_up) + b_up
        activation_wide, gelu_back = jax.vjp(partial(jax.nn.gelu, approximate=True), before_gelu)
        activation = activation_wide.astype(jnp.bfloat16)
        branch = (
            lax.psum_scatter(
                matmul(
                    lax.slice_in_dim(activation, 0, local_rows * lax.axis_size("tensor"), axis=0),
                    w_down,
                ),
                "tensor",
                scatter_dimension=0,
                tiled=True,
            )
            + b_down
        )
        output, norm_two_back = jax.vjp(layer_norm, hidden_one + branch, gain_two, shift_two)
        grad_two, grad_gain_two, grad_shift_two = norm_two_back(cotangent_rows.astype(jnp.float32))
        grad_branch = grad_two.astype(jnp.bfloat16)
        grad_b_down = jnp.sum(grad_branch.astype(jnp.float32), 0)
        branch_full = lax.all_gather(grad_branch, "tensor", axis=0, tiled=True)
        grad_w_down = jnp.einsum(
            "sf,sd->fd", activation, branch_full, preferred_element_type=jnp.float32
        )
        grad_act = jnp.einsum("sd,fd->sf", branch_full, w_down, preferred_element_type=jnp.float32)
        grad_before = gelu_back(grad_act)[0].astype(jnp.bfloat16)
        grad_b_up = jnp.sum(grad_before.astype(jnp.float32), 0)
        grad_w_up = jnp.einsum(
            "sd,sf->df", hidden_full, grad_before, preferred_element_type=jnp.float32
        )
        grad_hidden = (
            lax.psum_scatter(
                jnp.einsum(
                    "sf,df->sd", grad_before, w_up, preferred_element_type=jnp.float32
                ).astype(jnp.bfloat16),
                "tensor",
                scatter_dimension=0,
                tiled=True,
            ).astype(jnp.float32)
            + grad_two
        )
        grad_one, grad_gain_one, grad_shift_one = norm_one_back(grad_hidden)
        grad_attended = grad_one.astype(jnp.bfloat16)
        grad_b_out = jnp.sum(grad_attended.astype(jnp.float32), 0)
        attended_full = lax.all_gather(grad_attended, "tensor", axis=0, tiled=True)
        grad_w_out = jnp.einsum(
            "se,sd->ed", context, attended_full, preferred_element_type=jnp.float32
        )
        grad_context = jnp.einsum(
            "sd,ed->se", attended_full, w_out, preferred_element_type=jnp.float32
        )
        grad_context = grad_context.astype(jnp.bfloat16).reshape(length, local_heads, HEAD_DIM)
        grad_key_sum = jnp.zeros((length, local_heads, HEAD_DIM), jnp.float32)
        grad_value_sum = jnp.zeros((length, local_heads, HEAD_DIM), jnp.float32)
        query_grad_parts = []
        for block_index in range(block_total):
            first_row = block_index * block_rows
            masked, query_block = block_scores(first_row)
            attention = jnp.exp(masked - log_sums[:, first_row : first_row + block_rows])
            context_block = grad_context[first_row : first_row + block_rows]
            grad_weights = jnp.einsum(
                "qhd,khd->hqk", context_block, value_heads, preferred_element_type=jnp.float32
            )
            row_dot = jnp.sum(attention * grad_weights, -1, keepdims=True)
            grad_scores = (attention * (grad_weights - row_dot)).astype(jnp.bfloat16)
            query_grad_parts.append(
                jnp.einsum(
                    "hqk,khd->qhd", grad_scores, key_heads, preferred_element_type=jnp.float32
                )
                * score_scale
            )
            grad_key_sum = (
                grad_key_sum
                + jnp.einsum(
                    "hqk,qhd->khd", grad_scores, query_block, preferred_element_type=jnp.float32
                )
                * score_scale
            )
            grad_value_sum = grad_value_sum + jnp.einsum(
                "hqk,qhd->khd",
                attention.astype(jnp.bfloat16),
                context_block,
                preferred_element_type=jnp.float32,
            )
        grad_query = (
            jnp.concatenate(query_grad_parts, 0).reshape(length, local_width).astype(jnp.bfloat16)
        )
        grad_keys = grad_key_sum.reshape(length, local_width).astype(jnp.bfloat16)
        grad_values = grad_value_sum.reshape(length, local_width).astype(jnp.bfloat16)
        grad_w_query = jnp.einsum(
            "sd,se->de", inputs_full, grad_query, preferred_element_type=jnp.float32
        )
        grad_w_key = jnp.einsum(
            "sd,se->de", inputs_full, grad_keys, preferred_element_type=jnp.float32
        )
        grad_w_value = jnp.einsum(
            "sd,se->de", inputs_full, grad_values, preferred_element_type=jnp.float32
        )
        grad_b_query = jnp.sum(grad_query.astype(jnp.float32), 0)
        grad_b_value = jnp.sum(grad_values.astype(jnp.float32), 0)
        total = jnp.einsum("se,de->sd", grad_query, w_query, preferred_element_type=jnp.float32)
        total = total + jnp.einsum(
            "se,de->sd", grad_keys, w_key, preferred_element_type=jnp.float32
        )
        grad_input = (
            lax.psum_scatter(
                (
                    total
                    + jnp.einsum(
                        "se,de->sd", grad_values, w_value, preferred_element_type=jnp.float32
                    )
                ).astype(jnp.bfloat16),
                "tensor",
                scatter_dimension=0,
                tiled=True,
            ).astype(jnp.float32)
            + grad_one
        )
        split_grads = (
            grad_w_query,
            grad_w_key,
            grad_w_value,
            grad_b_query,
            grad_b_value,
            grad_w_out,
            grad_w_up,
            grad_b_up,
            grad_w_down,
        )
        shared_grads = (
            grad_b_out,
            grad_gain_one,
            grad_shift_one,
            grad_b_down,
            grad_gain_two,
            grad_shift_two,
        )
        return (output.astype(jnp.bfloat16), grad_input, split_grads, shared_grads)

    shared_zero = tuple((jnp.zeros(param.shape, jnp.float32) for param in shared_params))
    split_zero = tuple((jnp.zeros(param.shape, jnp.float32) for param in split_params))

    def micro_step(running, sequence_item):
        split_running, shared_running = running
        output_rows, input_grad, split_new, shared_new = micro_pass(*sequence_item)
        return (
            (add_tuple(split_running, split_new), add_tuple(shared_running, shared_new)),
            (output_rows, input_grad),
        )

    (split_total, shared_total), (outputs, grad_inputs) = lax.scan(
        micro_step, (split_zero, shared_zero), (inputs, segment_ids, cotangent)
    )
    split_total = lax.psum(split_total, "dp")
    shared_total = lax.psum(shared_total, ("dp", "tensor"))
    return (
        outputs,
        grad_inputs,
        split_total[0],
        split_total[1],
        split_total[2],
        split_total[3],
        split_total[4],
        split_total[5],
        shared_total[0],
        shared_total[1],
        shared_total[2],
        split_total[6],
        split_total[7],
        split_total[8],
        shared_total[3],
        shared_total[4],
        shared_total[5],
    )


def solution(mesh):
    return jax.shard_map(
        shards,
        mesh=mesh,
        in_specs=(
            P("dp", "tensor", None),
            P("dp", None),
            P("dp", "tensor", None),
            P(None, "tensor"),
            P(None, "tensor"),
            P(None, "tensor"),
            P("tensor"),
            P("tensor"),
            P("tensor", None),
            P(),
            P(),
            P(),
            P(None, "tensor"),
            P("tensor"),
            P("tensor", None),
            P(),
            P(),
            P(),
        ),
        out_specs=(
            P("dp", "tensor", None),
            P("dp", "tensor", None),
            P(None, "tensor"),
            P(None, "tensor"),
            P(None, "tensor"),
            P("tensor"),
            P("tensor"),
            P("tensor", None),
            P(),
            P(),
            P(),
            P(None, "tensor"),
            P("tensor"),
            P("tensor", None),
            P(),
            P(),
            P(),
        ),
        check_vma=False,
    )
```

profile of v0, /device:TPU:0, one launch (start us, length us, event | category | flops | bytes accessed | tf_op | source)
XLA Modules:
  0.0 850.5 jit_solution(10701467039942514248)
XLA Ops:
  8.2 586.2 %while.45 = (s32[]{:T(128)}, f32[768,192]{0,1:T(8,128)}, f32[768,192]{0,1:T(8,128)}, f32[768,192]{0,1:T(8,128)}, f32[192]{0:T(256)}, /*index=5*/f32[192]{0:T(256...) while((s32[]{:T(128)}, f32[768,192]{0,1:T(8,128)}, ...), condition=%wide.region_28.29_spmd.clone, body=%wide.region_0.28_spmd.clone.sunk | while | flops 13402836992 | bytes 479719552 | solution.py:254
  12.3 20.7 %all-gather.9.cloned.1.call-done = bf16[1,1024,768]{2,1,0:T(8,128)(2,1)} async-done(((bf16[1,256,768]{2,1,0:T(8,128)(2,1)}), bf16[1,1024,768]{2,1,0:T(8,128)(2,1)}) %all-gather.9.cloned.1.call-update) | async-done | bytes 1572880 | tf_op jit(solution)/shard_map/while/body/eval_jaxpr/all_gather | solution.py:61
  33.0 2.3 fusion.288
  48.4 2.3 fusion.297
  50.7 38.0 %reduce-scatter.5.cloned.1.call-done = f32[256,768]{1,0:T(8,128)} async-done(((f32[1024,768]{1,0:T(8,128)}), f32[256,768]{1,0:T(8,128)}) %reduce-scatter.5.cloned.1.call-update) | async-done | bytes 786448 | tf_op jit(solution)/shard_map/while/body/eval_jaxpr/reduce_scatter | solution.py:99
  92.0 19.7 %all-gather.11.cloned.1.call-done = bf16[1024,768]{1,0:T(8,128)(2,1)} async-done(((bf16[256,768]{1,0:T(8,128)(2,1)}), bf16[1024,768]{1,0:T(8,128)(2,1)}) %all-gather.11.cloned.1.call-update) | async-done | bytes 1572880 | tf_op jit(solution)/shard_map/while/body/eval_jaxpr/all_gather | solution.py:104
  111.8 3.2 fusion.301
  116.7 3.8 fusion.302
  120.5 38.0 %reduce-scatter.7.cloned.1.call-done = f32[256,768]{1,0:T(8,128)} async-done(((f32[1024,768]{1,0:T(8,128)}), f32[256,768]{1,0:T(8,128)}) %reduce-scatter.7.cloned.1.call-update) | async-done | bytes 786448 | tf_op jit(solution)/shard_map/while/body/eval_jaxpr/reduce_scatter | solution.py:109
  166.1 19.7 %all-gather.13.cloned.1.call-done = bf16[1024,768]{1,0:T(8,128)(2,1)} async-done(((bf16[256,768]{1,0:T(8,128)(2,1)}), bf16[1024,768]{1,0:T(8,128)(2,1)}) %all-gather.13.cloned.1.call-update) | async-done | bytes 1572880 | tf_op jit(solution)/shard_map/while/body/eval_jaxpr/all_gather | solution.py:124
  185.8 6.4 convert_reduce_fusion.13
  193.4 2.6 convolution_convert_fusion.4
  196.1 28.2 %reduce-scatter.9.cloned.1.call-done = bf16[256,768]{1,0:T(8,128)(2,1)} async-done(((bf16[1024,768]{1,0:T(8,128)(2,1)}), bf16[256,768]{1,0:T(8,128)(2,1)}) %reduce-scatter.9.cloned.1.call-update) | async-done | bytes 393232 | tf_op jit(solution)/shard_map/while/body/eval_jaxpr/reduce_scatter | solution.py:135
  224.2 2.3 multiply_reduce_fusion.13
  237.4 13.7 %all-gather.15.cloned.1.call-done = bf16[1024,768]{1,0:T(8,128)(2,1)} async-done(((bf16[256,768]{1,0:T(8,128)(2,1)}), bf16[1024,768]{1,0:T(8,128)(2,1)}) %all-gather.15.cloned.1.call-update) | async-done | bytes 1572880 | tf_op jit(solution)/shard_map/while/body/eval_jaxpr/all_gather | solution.py:148
  251.1 2.1 convolution_convert_fusion.5
  253.3 3.9 multiply_reduce_fusion.15
  272.5 4.9 select_add_fusion.20
  277.5 3.4 select_add_fusion.22
  281.2 2.8 convolution_add_fusion.3
  287.6 13.0 %reduce-scatter.11.cloned.1.call-done = bf16[256,768]{1,0:T(8,128)(2,1)} async-done(((bf16[1024,768]{1,0:T(8,128)(2,1)}), bf16[256,768]{1,0:T(8,128)(2,1)}) %reduce-scatter.11.cloned.1.call-update) | async-done | bytes 393232 | tf_op jit(solution)/shard_map/while/body/eval_jaxpr/reduce_scatter | solution.py:209
  300.6 2.0 bitcast_dynamic-update-slice_fusion.2
  306.7 18.0 %all-gather.9.cloned.1.call-done = bf16[1,1024,768]{2,1,0:T(8,128)(2,1)} async-done(((bf16[1,256,768]{2,1,0:T(8,128)(2,1)}), bf16[1,1024,768]{2,1,0:T(8,128)(2,1)}) %all-gather.9.cloned.1.call-update) | async-done | bytes 1572880 | tf_op jit(solution)/shard_map/while/body/eval_jaxpr/all_gather | solution.py:61
  324.6 2.3 fusion.288
  340.0 2.3 fusion.297
  342.4 38.0 %reduce-scatter.5.cloned.1.call-done = f32[256,768]{1,0:T(8,128)} async-done(((f32[1024,768]{1,0:T(8,128)}), f32[256,768]{1,0:T(8,128)}) %reduce-scatter.5.cloned.1.call-update) | async-done | bytes 786448 | tf_op jit(solution)/shard_map/while/body/eval_jaxpr/reduce_scatter | solution.py:99
  383.7 19.7 %all-gather.11.cloned.1.call-done = bf16[1024,768]{1,0:T(8,128)(2,1)} async-done(((bf16[256,768]{1,0:T(8,128)(2,1)}), bf16[1024,768]{1,0:T(8,128)(2,1)}) %all-gather.11.cloned.1.call-update) | async-done | bytes 1572880 | tf_op jit(solution)/shard_map/while/body/eval_jaxpr/all_gather | solution.py:104
  403.5 3.2 fusion.301
  408.4 3.8 fusion.302
  412.2 38.0 %reduce-scatter.7.cloned.1.call-done = f32[256,768]{1,0:T(8,128)} async-done(((f32[1024,768]{1,0:T(8,128)}), f32[256,768]{1,0:T(8,128)}) %reduce-scatter.7.cloned.1.call-update) | async-done | bytes 786448 | tf_op jit(solution)/shard_map/while/body/eval_jaxpr/reduce_scatter | solution.py:109
  457.8 19.7 %all-gather.13.cloned.1.call-done = bf16[1024,768]{1,0:T(8,128)(2,1)} async-done(((bf16[256,768]{1,0:T(8,128)(2,1)}), bf16[1024,768]{1,0:T(8,128)(2,1)}) %all-gather.13.cloned.1.call-update) | async-done | bytes 1572880 | tf_op jit(solution)/shard_map/while/body/eval_jaxpr/all_gather | solution.py:124
  477.5 6.4 convert_reduce_fusion.13
  485.1 2.6 convolution_convert_fusion.4
  487.8 28.2 %reduce-scatter.9.cloned.1.call-done = bf16[256,768]{1,0:T(8,128)(2,1)} async-done(((bf16[1024,768]{1,0:T(8,128)(2,1)}), bf16[256,768]{1,0:T(8,128)(2,1)}) %reduce-scatter.9.cloned.1.call-update) | async-done | bytes 393232 | tf_op jit(solution)/shard_map/while/body/eval_jaxpr/reduce_scatter | solution.py:135
  515.9 2.3 multiply_reduce_fusion.13
  529.8 13.0 %all-gather.15.cloned.1.call-done = bf16[1024,768]{1,0:T(8,128)(2,1)} async-done(((bf16[256,768]{1,0:T(8,128)(2,1)}), bf16[1024,768]{1,0:T(8,128)(2,1)}) %all-gather.15.cloned.1.call-update) | async-done | bytes 1572880 | tf_op jit(solution)/shard_map/while/body/eval_jaxpr/all_gather | solution.py:148
  542.8 2.1 convolution_convert_fusion.5
  544.9 3.9 multiply_reduce_fusion.15
  564.2 5.6 select_add_fusion.20
  569.9 5.2 select_add_fusion.22
  575.5 2.9 convolution_add_fusion.3
  580.7 2.4 fusion.314
  583.0 9.3 %reduce-scatter.11.cloned.1.call-done = bf16[256,768]{1,0:T(8,128)(2,1)} async-done(((bf16[1024,768]{1,0:T(8,128)(2,1)}), bf16[256,768]{1,0:T(8,128)(2,1)}) %reduce-scatter.11.cloned.1.call-update) | async-done | bytes 393232 | tf_op jit(solution)/shard_map/while/body/eval_jaxpr/reduce_scatter | solution.py:209
  592.4 2.0 bitcast_dynamic-update-slice_fusion.2
  595.1 23.1 %all-reduce.1 = (f32[192]{0:T(256)}, f32[192]{0:T(256)}, f32[768]{0:T(1024)}) all-reduce(f32[192]{0:T(256)S(1)} %copy-done.62, f32[192]{0:T(256)S(1)} %copy-done.59, f32[768]{0:T(1024)S(1)} %copy-done.43), channel_id=1, replica_groups=mesh['dp'=8,'tensor'=4] {'dp'}, use_global_device_ids=true, to_apply=%region_32.33 | all-reduce | flops 1152 | bytes 9216 | tf_op jit(solution)/shard_map/psum | solution.py:257
  618.2 41.1 %all-reduce = (f32[768]{0:T(1024)}, f32[768]{0:T(1024)}, f32[768]{0:T(1024)}, f32[768]{0:T(1024)}, f32[768]{0:T(1024)}, /*index=5*/f32[768]{0:T(1024)}) all-reduce(f32[768]{0:T(1024)S(1)} %copy-done.55, f32[768]{0:T(1024)S(1)} %copy-done.52, f32[768]{0:T(1024)S(1)} %copy-done.49, ...), channel_id=1, replica_groups=mesh['dp'=8,'tensor'=4] {'dp','tensor'}, use_global_device_ids=true, to_apply=%region_35.36 | all-reduce | flops 4608 | bytes 36864 | tf_op jit(solution)/shard_map/psum | solution.py:258
  659.3 174.6 %all-reduce.5.cloned.1.call-done = (f32[768,192]{0,1:T(8,128)}, f32[768,192]{0,1:T(8,128)}, f32[768,192]{0,1:T(8,128)}, f32[192,768]{1,0:T(8,128)}, f32[768,768]{1,0:T(8,128)}, /*index=5*/f32[768,768]{1,0:T(8,128)}) async-done(((f32[768,192]{0,1:T(8,128)}, f32[768,192]{0,1:T(8,128)}, f32[768,192]{0,1:T(8,128)}, f32[192,768]{1,0:T(8,128)}, f32[768,768]{1,0:T(8,128)}, /*index=5*/f32[768,768]{1,0:T(8,128)}), ...) | async-done | bytes 7077904 | tf_op jit(solution)/shard_map/psum | solution.py:257
  833.9 2.1 copy.97
  (461 shorter events, 128.5 us)
Async XLA Ops:
  8.2 27.1 %copy-start.21 = (bf16[768,192]{0,1:T(8,128)(2,1)S(1)}, bf16[768,192]{0,1:T(8,128)(2,1)}, u32[]{:S(2)}) copy-start(bf16[768,192]{0,1:T(8,128)(2,1)} %get-tuple-element.1134) | copy-start | bytes 884740 | tf_op jit(solution)/shard_map/while
  8.2 24.8 %all-gather.9.cloned.1.call-start = ((), (), s32[]{:S(2)}) async-start(), calls=%async_computation.5 | async-start | bytes 1966080 | tf_op jit(solution)/shard_map/while/body/eval_jaxpr/all_gather | solution.py:61
  10.1 78.6 %reduce-scatter.5.cloned.1.call-start = ((), (), s32[]{:S(2)}) async-start(), calls=%async_computation.6 | async-start | bytes 3932160 | tf_op jit(solution)/shard_map/while/body/eval_jaxpr/reduce_scatter | solution.py:99
  35.3 6.5 copy-start.10
  48.4 40.3 %copy-start.18 = (bf16[2,256,768]{2,1,0:T(8,128)(2,1)S(1)}, bf16[2,256,768]{2,1,0:T(8,128)(2,1)}, u32[]{:S(2)}) copy-start(bf16[2,256,768]{2,1,0:T(8,128)(2,1)} %get-tuple-element.1133) | copy-start | bytes 2359300 | tf_op jit(solution)/shard_map/while
  50.6 61.1 %all-gather.11.cloned.1.call-start = ((), (), s32[]{:S(2)}) async-start(), calls=%async_computation.7 | async-start | bytes 1966080 | tf_op jit(solution)/shard_map/while/body/eval_jaxpr/all_gather | solution.py:104
  90.0 25.0 %copy-start.27 = (f32[256]{0:T(256)}, f32[256]{0:T(256)S(1)}, u32[]{:S(2)}) copy-start(f32[256]{0:T(256)S(1)} %broadcast_multiply_fusion.4) | copy-start | bytes 3076 | tf_op jit(solution)/shard_map/while
  90.3 24.8 %copy-start.38 = (f32[256]{0:T(256)}, f32[256]{0:T(256)S(1)}, u32[]{:S(2)}) copy-start(f32[256]{0:T(256)S(1)} %multiply_reduce_fusion.11) | copy-start | bytes 3076 | tf_op jit(solution)/shard_map/while
  90.3 24.7 %copy-start.30 = (f32[256]{0:T(256)}, f32[256]{0:T(256)S(1)}, u32[]{:S(2)}) copy-start(f32[256]{0:T(256)S(1)} %fusion.299) | copy-start | bytes 3076 | tf_op jit(solution)/shard_map/while
  92.0 66.5 %reduce-scatter.7.cloned.1.call-start = ((), (), s32[]{:S(2)}) async-start(), calls=%async_computation.8 | async-start | bytes 3932160 | tf_op jit(solution)/shard_map/while/body/eval_jaxpr/reduce_scatter | solution.py:109
  120.5 65.4 %all-gather.13.cloned.1.call-start = ((), (), s32[]{:S(2)}) async-start(), calls=%async_computation.9 | async-start | bytes 1966080 | tf_op jit(solution)/shard_map/while/body/eval_jaxpr/all_gather | solution.py:124
  160.0 6.0 copy-start.31
  166.0 58.2 %reduce-scatter.9.cloned.1.call-start = ((), (), s32[]{:S(2)}) async-start(), calls=%async_computation.10 | async-start | bytes 1966080 | tf_op jit(solution)/shard_map/while/body/eval_jaxpr/reduce_scatter | solution.py:135
  185.8 7.6 copy-start.64
  196.0 55.1 %all-gather.15.cloned.1.call-start = ((), (), s32[]{:S(2)}) async-start(), calls=%async_computation.11 | async-start | bytes 1966080 | tf_op jit(solution)/shard_map/while/body/eval_jaxpr/all_gather | solution.py:148
  229.8 23.4 %copy-start.13 = (bf16[1024,192]{0,1:T(8,128)(2,1)S(1)}, bf16[1024,192]{0,1:T(8,128)(2,1)}, u32[]{:S(2)}) copy-start(bf16[1024,192]{0,1:T(8,128)(2,1)} %copy-done.12) | copy-start | bytes 1179652 | tf_op jit(solution)/shard_map/while
  231.3 69.3 %reduce-scatter.11.cloned.1.call-start = ((), (), s32[]{:S(2)}) async-start(), calls=%async_computation.12 | async-start | bytes 1966080 | tf_op jit(solution)/shard_map/while/body/eval_jaxpr/reduce_scatter | solution.py:209
  284.7 15.9 %copy-start.5 = (f32[256,768]{1,0:T(8,128)S(1)}, f32[256,768]{1,0:T(8,128)}, u32[]{:S(2)}) copy-start(f32[256,768]{1,0:T(8,128)} %copy-done.4) | copy-start | bytes 2359300 | tf_op jit(solution)/shard_map/while
  284.7 15.9 %copy-start.40 = (f32[256]{0:T(256)S(1)}, f32[256]{0:T(256)}, u32[]{:S(2)}) copy-start(f32[256]{0:T(256)} %copy-done.39) | copy-start | bytes 3076 | tf_op jit(solution)/shard_map/while
  302.6 24.4 %copy-start.21 = (bf16[768,192]{0,1:T(8,128)(2,1)S(1)}, bf16[768,192]{0,1:T(8,128)(2,1)}, u32[]{:S(2)}) copy-start(bf16[768,192]{0,1:T(8,128)(2,1)} %get-tuple-element.1134) | copy-start | bytes 884740 | tf_op jit(solution)/shard_map/while
  302.6 22.0 %all-gather.9.cloned.1.call-start = ((), (), s32[]{:S(2)}) async-start(), calls=%async_computation.5 | async-start | bytes 1966080 | tf_op jit(solution)/shard_map/while/body/eval_jaxpr/all_gather | solution.py:61
  304.5 75.9 %reduce-scatter.5.cloned.1.call-start = ((), (), s32[]{:S(2)}) async-start(), calls=%async_computation.6 | async-start | bytes 3932160 | tf_op jit(solution)/shard_map/while/body/eval_jaxpr/reduce_scatter | solution.py:99
  327.0 6.5 copy-start.10
  340.0 40.3 %copy-start.18 = (bf16[2,256,768]{2,1,0:T(8,128)(2,1)S(1)}, bf16[2,256,768]{2,1,0:T(8,128)(2,1)}, u32[]{:S(2)}) copy-start(bf16[2,256,768]{2,1,0:T(8,128)(2,1)} %get-tuple-element.1133) | copy-start | bytes 2359300 | tf_op jit(solution)/shard_map/while
  342.3 61.1 %all-gather.11.cloned.1.call-start = ((), (), s32[]{:S(2)}) async-start(), calls=%async_computation.7 | async-start | bytes 1966080 | tf_op jit(solution)/shard_map/while/body/eval_jaxpr/all_gather | solution.py:104
  381.7 25.0 %copy-start.27 = (f32[256]{0:T(256)}, f32[256]{0:T(256)S(1)}, u32[]{:S(2)}) copy-start(f32[256]{0:T(256)S(1)} %broadcast_multiply_fusion.4) | copy-start | bytes 3076 | tf_op jit(solution)/shard_map/while
  381.9 24.8 %copy-start.38 = (f32[256]{0:T(256)}, f32[256]{0:T(256)S(1)}, u32[]{:S(2)}) copy-start(f32[256]{0:T(256)S(1)} %multiply_reduce_fusion.11) | copy-start | bytes 3076 | tf_op jit(solution)/shard_map/while
  382.0 24.7 %copy-start.30 = (f32[256]{0:T(256)}, f32[256]{0:T(256)S(1)}, u32[]{:S(2)}) copy-start(f32[256]{0:T(256)S(1)} %fusion.299) | copy-start | bytes 3076 | tf_op jit(solution)/shard_map/while
  383.7 66.5 %reduce-scatter.7.cloned.1.call-start = ((), (), s32[]{:S(2)}) async-start(), calls=%async_computation.8 | async-start | bytes 3932160 | tf_op jit(solution)/shard_map/while/body/eval_jaxpr/reduce_scatter | solution.py:109
  412.1 65.4 %all-gather.13.cloned.1.call-start = ((), (), s32[]{:S(2)}) async-start(), calls=%async_computation.9 | async-start | bytes 1966080 | tf_op jit(solution)/shard_map/while/body/eval_jaxpr/all_gather | solution.py:124
  451.7 6.0 copy-start.31
  457.7 58.2 %reduce-scatter.9.cloned.1.call-start = ((), (), s32[]{:S(2)}) async-start(), calls=%async_computation.10 | async-start | bytes 1966080 | tf_op jit(solution)/shard_map/while/body/eval_jaxpr/reduce_scatter | solution.py:135
  477.5 7.6 copy-start.64
  487.7 55.1 %all-gather.15.cloned.1.call-start = ((), (), s32[]{:S(2)}) async-start(), calls=%async_computation.11 | async-start | bytes 1966080 | tf_op jit(solution)/shard_map/while/body/eval_jaxpr/all_gather | solution.py:148
  521.5 23.4 %copy-start.13 = (bf16[1024,192]{0,1:T(8,128)(2,1)S(1)}, bf16[1024,192]{0,1:T(8,128)(2,1)}, u32[]{:S(2)}) copy-start(bf16[1024,192]{0,1:T(8,128)(2,1)} %copy-done.12) | copy-start | bytes 1179652 | tf_op jit(solution)/shard_map/while
  523.0 69.4 %reduce-scatter.11.cloned.1.call-start = ((), (), s32[]{:S(2)}) async-start(), calls=%async_computation.12 | async-start | bytes 1966080 | tf_op jit(solution)/shard_map/while/body/eval_jaxpr/reduce_scatter | solution.py:209
  564.1 5.7 copy-start.42
  579.1 13.3 %copy-start.5 = (f32[256,768]{1,0:T(8,128)S(1)}, f32[256,768]{1,0:T(8,128)}, u32[]{:S(2)}) copy-start(f32[256,768]{1,0:T(8,128)} %copy-done.4) | copy-start | bytes 2359300 | tf_op jit(solution)/shard_map/while
  579.1 13.3 %copy-start.40 = (f32[256]{0:T(256)S(1)}, f32[256]{0:T(256)}, u32[]{:S(2)}) copy-start(f32[256]{0:T(256)} %copy-done.39) | copy-start | bytes 3076 | tf_op jit(solution)/shard_map/while
  594.4 239.5 %all-reduce.5.cloned.1.call-start = ((), (), s32[]{:S(2)}) async-start(), calls=%async_computation.4 | async-start | bytes 14155776 | tf_op jit(solution)/shard_map/psum | solution.py:257
  594.4 23.8 %copy-start.44 = (f32[768]{0:T(1024)S(1)}, f32[768]{0:T(1024)}, u32[]{:S(2)}) copy-start(f32[768]{0:T(1024)} %get-tuple-element.486) | copy-start | bytes 9220
  594.4 23.8 %copy-start.45 = (f32[768]{0:T(1024)S(1)}, f32[768]{0:T(1024)}, u32[]{:S(2)}) copy-start(f32[768]{0:T(1024)} %get-tuple-element.485) | copy-start | bytes 9220
  594.4 23.7 %copy-start.46 = (f32[768]{0:T(1024)S(1)}, f32[768]{0:T(1024)}, u32[]{:S(2)}) copy-start(f32[768]{0:T(1024)} %get-tuple-element.484) | copy-start | bytes 9220
  594.4 23.7 %copy-start.49 = (f32[768]{0:T(1024)S(1)}, f32[768]{0:T(1024)}, u32[]{:S(2)}) copy-start(f32[768]{0:T(1024)} %get-tuple-element.480) | copy-start | bytes 9220
  594.5 23.7 %copy-start.52 = (f32[768]{0:T(1024)S(1)}, f32[768]{0:T(1024)}, u32[]{:S(2)}) copy-start(f32[768]{0:T(1024)} %get-tuple-element.479) | copy-start | bytes 9220
  594.5 23.7 %copy-start.55 = (f32[768]{0:T(1024)S(1)}, f32[768]{0:T(1024)}, u32[]{:S(2)}) copy-start(f32[768]{0:T(1024)} %get-tuple-element.478) | copy-start | bytes 9220
  833.9 5.9 copy-start.32
  833.9 6.7 copy-start.26
  (109 other events, 320.4 us)
Sparse Core Ops, SparseCore 0:
  10.6 22.3 all-gather.8
  50.8 37.8 reduce-scatter.4
  92.1 19.6 all-gather.10
  120.6 37.8 reduce-scatter.6
  166.1 19.6 all-gather.12
  196.1 28.0 reduce-scatter.8
  231.4 19.6 all-gather.14
  272.5 28.0 reduce-scatter.10
  305.0 19.6 all-gather.8
  342.5 37.8 reduce-scatter.4
  383.8 19.6 all-gather.10
  412.3 37.8 reduce-scatter.6
  457.8 19.6 all-gather.12
  487.8 28.0 reduce-scatter.8
  523.1 19.6 all-gather.14
  564.2 28.0 reduce-scatter.10
Sparse Core Ops, SparseCore 1:
  601.1 232.7 all-reduce.4
where the time goes:
time: 852 us; the launch traced here: 851 us
  waiting for transfers between devices  550 us (65%)
  matrix products  121 us (14%)
  blocking collectives  64.2 us (8%)
  other arithmetic  61.8 us (7%)
  local copies, waits for them, and re-layouts  35.4 us (4%)
  between operations  15.4 us (2%)
    psum x1, waiting for transfers between devices, shards(): split_total = lax.psum(split_total, 'dp')  175 us
    reduce_scatter x2, waiting for transfers between devices, micro_pass(): lax.psum_scatter(matmul(context, w_out), 'tensor', scatter_dimension=0, t...  76 us
    reduce_scatter x2, waiting for transfers between devices, micro_pass(): lax.psum_scatter(matmul(lax.slice_in_dim(activation, 0, local_rows * lax....  76 us
    reduce_scatter x2, waiting for transfers between devices, micro_pass(): lax.psum_scatter(jnp.einsum('sf,df->sd', grad_before, w_up, preferred_ele...  56.3 us
    psum x1, blocking collectives, shards(): shared_total = lax.psum(shared_total, ('dp', 'tensor'))  41.1 us
    all_gather x2, waiting for transfers between devices, micro_pass(): lax.all_gather(hidden_one.astype(jnp.bfloat16), 'tensor', axis=0, tiled=T...  39.5 us
    all_gather x2, waiting for transfers between devices, micro_pass(): branch_full = lax.all_gather(grad_branch, 'tensor', axis=0, tiled=True)  39.5 us
    all_gather x2, waiting for transfers between devices, micro_pass(): inputs_full = lax.all_gather(input_rows, 'tensor', axis=0, tiled=True)  38.7 us
  transfers between devices with their start and end apart: 17, of which 17 were waited for; matrix products, arithmetic and copies ran while one was open for 6% of the time, Pallas kernels for 0%

commit v1 on v0

v1 whole, which is shorter than its diff:
```python
import math

import jax
import jax.numpy as jnp
from jax import lax
from jax.sharding import PartitionSpec as P

HEAD_DIM = 64
LAYER_EPSILON = 1e-05
BF = jnp.bfloat16
F32 = jnp.float32


def dot(left, right, contract):
    return lax.dot_general(left, right, (contract, ((), ())), preferred_element_type=F32)


def mm(left, right):
    return dot(left, right, ((1,), (0,)))


def mm_t(left, right):
    return dot(left, right, ((1,), (1,)))


def t_mm(left, right):
    return dot(left, right, ((0,), (0,)))


def normalize(rows):
    centred = rows - jnp.mean(rows, -1, keepdims=True)
    inverse = lax.rsqrt(jnp.mean(centred * centred, -1, keepdims=True) + LAYER_EPSILON)
    return centred * inverse, inverse


def norm_backward(grad, gain, normal, inverse):
    scaled = grad * gain
    mean = jnp.mean(scaled, -1, keepdims=True)
    mean_z = jnp.mean(scaled * normal, -1, keepdims=True)
    return inverse * (scaled - mean - normal * mean_z), jnp.sum(grad * normal, 0), jnp.sum(grad, 0)


def gelu_pair(u):
    root = math.sqrt(2 / math.pi)
    t = jnp.tanh(root * (u + 0.044715 * u * u * u))
    value = 0.5 * u * (1 + t)
    slope = 0.5 * (1 + t) + 0.5 * u * (1 - t * t) * root * (1 + 3 * 0.044715 * u * u)
    return value, slope


def attention_forward(query, keys, values, seg_q, seg_k):
    scores = jnp.einsum("qhd,khd->hqk", query, keys, preferred_element_type=F32) / math.sqrt(HEAD_DIM)
    masked = jnp.where((seg_q[:, None] == seg_k[None, :])[None], scores, -1e30)
    top = jnp.max(masked, -1, keepdims=True)
    exponent = jnp.exp(masked - top)
    total = jnp.sum(exponent, -1, keepdims=True)
    weights = (exponent / total).astype(BF)
    context = jnp.einsum("hqk,khd->qhd", weights, values, preferred_element_type=F32)
    return context.astype(BF), top + jnp.log(total)


def attention_backward(query, keys, values, seg_q, seg_k, logsum, grad):
    scale = 1 / math.sqrt(HEAD_DIM)
    scores = jnp.einsum("qhd,khd->hqk", query, keys, preferred_element_type=F32) * scale
    masked = jnp.where((seg_q[:, None] == seg_k[None, :])[None], scores, -1e30)
    weights = jnp.exp(masked - logsum)
    grad_weights = jnp.einsum("qhd,khd->hqk", grad, values, preferred_element_type=F32)
    row = jnp.sum(weights * grad_weights, -1, keepdims=True)
    grad_scores = (weights * (grad_weights - row)).astype(BF)
    grad_query = jnp.einsum("hqk,khd->qhd", grad_scores, keys, preferred_element_type=F32) * scale
    grad_keys = jnp.einsum("hqk,qhd->khd", grad_scores, query, preferred_element_type=F32) * scale
    grad_values = jnp.einsum("hqk,qhd->khd", weights.astype(BF), grad, preferred_element_type=F32)
    return grad_query.astype(BF), grad_keys, grad_values


def shards(
    inputs,
    segment_ids,
    cotangent,
    w_query,
    w_key,
    w_value,
    b_query,
    b_value,
    w_out,
    b_out,
    gain_one,
    shift_one,
    w_up,
    b_up,
    w_down,
    b_down,
    gain_two,
    shift_two,
):
    ranks = lax.axis_size("tensor")
    rank = lax.axis_index("tensor")
    which = rank % 2
    rows = inputs.shape[1]
    half = 2 * rows
    width = w_query.shape[1]
    hidden_width = w_up.shape[1]
    model = inputs.shape[2]

    def inner(x):
        return lax.ppermute(x, "tensor", [(i, i ^ 1) for i in range(ranks)])

    def outer(x):
        return lax.ppermute(x, "tensor", [(i, i ^ 2) for i in range(ranks)])

    def to_sequence(x):
        kept = jnp.where(which == 0, x[0], x[1])
        got = inner(jnp.where(which == 0, x[1], x[0]))
        return jnp.where(which == 0, jnp.concatenate([kept, got]), jnp.concatenate([got, kept]))

    def from_sequence(x):
        low, high = x[:rows], x[rows:]
        kept = jnp.where(which == 0, low, high)
        got = inner(jnp.where(which == 0, high, low))
        return jnp.where(which == 0, jnp.stack([kept, got]), jnp.stack([got, kept]))

    own_in = to_sequence(inputs)
    other_in = outer(own_in)
    own_cot = to_sequence(cotangent).astype(F32)

    def both(x, axis):
        return jnp.concatenate([x, inner(x)], axis)

    wqkv = both(jnp.concatenate([w_query, w_key, w_value], 1)[None], 0)
    wqkv = wqkv.reshape(2, model, 3, width).transpose(1, 2, 0, 3).reshape(model, 3 * 2 * width)
    bias = both(jnp.stack([b_query, b_value])[None], 0).transpose(1, 0, 2).reshape(2, 2 * width)
    bias_qkv = jnp.concatenate([bias[0], jnp.zeros((2 * width,), F32), bias[1]])
    w_out2 = both(w_out, 0)
    w_up2 = both(w_up, 1)
    b_up2 = both(b_up, 0)
    w_down2 = both(w_down, 0)

    segments = jnp.where(which == 0, segment_ids[0], segment_ids[1])
    first = jnp.where(rank // 2 == 0, segments[:half], segments[half:])
    second = jnp.where(rank // 2 == 0, segments[half:], segments[:half])
    seg = jnp.concatenate([first, second])

    heads = 2 * width // HEAD_DIM

    def project(x):
        return (mm(x, wqkv) + bias_qkv).astype(BF)

    qkv = [project(own_in), project(other_in)]

    def split(x):
        return [x[:, i * 2 * width : (i + 1) * 2 * width].reshape(-1, heads, HEAD_DIM) for i in range(3)]

    pieces = [split(x) for x in qkv]
    keys = jnp.concatenate([pieces[0][1], pieces[1][1]])
    values = jnp.concatenate([pieces[0][2], pieces[1][2]])
    context_other, log_other = attention_forward(pieces[1][0], keys, values, second, seg)
    context_other = context_other.reshape(half, 2 * width)
    got = outer(mm(context_other, w_out2).astype(BF))
    context_own, log_own = attention_forward(pieces[0][0], keys, values, first, seg)
    context_own = context_own.reshape(half, 2 * width)
    attended = mm(context_own, w_out2) + got.astype(F32) + b_out
    normal_one, inverse_one = normalize(own_in.astype(F32) + attended)
    hidden_one = normal_one * gain_one + shift_one
    low_own = hidden_one.astype(BF)
    low_other = outer(low_own)

    def feed(low):
        value, slope = gelu_pair(mm(low, w_up2) + b_up2)
        return value.astype(BF), slope

    act_own, slope_own = feed(low_own)
    act_other, slope_other = feed(low_other)
    got = outer(mm(act_other, w_down2).astype(BF))
    branch = mm(act_own, w_down2) + got.astype(F32) + b_down
    normal_two, inverse_two = normalize(hidden_one + branch)
    output = (normal_two * gain_two + shift_two).astype(BF)

    grad_two, grad_gain_two, grad_shift_two = norm_backward(own_cot, gain_two, normal_two, inverse_two)
    gb_own = grad_two.astype(BF)
    grad_b_down = jnp.sum(gb_own.astype(F32), 0)
    gb_other = outer(gb_own)
    before_own = (mm_t(gb_own, w_down2) * slope_own).astype(BF)
    before_other = (mm_t(gb_other, w_down2) * slope_other).astype(BF)
    got = outer(mm_t(before_other, w_up2).astype(BF))
    grad_w_down = t_mm(act_own, gb_own) + t_mm(act_other, gb_other)
    grad_w_up = t_mm(low_own, before_own) + t_mm(low_other, before_other)
    grad_b_up = jnp.sum(before_own.astype(F32), 0) + jnp.sum(before_other.astype(F32), 0)
    grad_hidden = mm_t(before_own, w_up2) + got.astype(F32) + grad_two
    grad_one, grad_gain_one, grad_shift_one = norm_backward(grad_hidden, gain_one, normal_one, inverse_one)
    ga_own = grad_one.astype(BF)
    grad_b_out = jnp.sum(ga_own.astype(F32), 0)
    ga_other = outer(ga_own)

    def pair_sum(mine, theirs):
        return mine + inner(theirs.astype(BF)).astype(F32)

    grad_w_up = pair_sum(grad_w_up[:, :hidden_width], grad_w_up[:, hidden_width:])
    grad_w_down = pair_sum(grad_w_down[:hidden_width], grad_w_down[hidden_width:])
    feed_flat = jnp.concatenate([grad_w_up.astype(BF), grad_w_down.astype(BF)])
    feed_flat = lax.psum(feed_flat, "dp")

    gc_own = mm_t(ga_own, w_out2).astype(BF)
    gc_other = mm_t(ga_other, w_out2).astype(BF)
    grad_w_out = t_mm(context_own, ga_own) + t_mm(context_other, ga_other)
    shaped = (half, heads, HEAD_DIM)
    gq_own, gk_a, gv_a = attention_backward(
        pieces[0][0], keys, values, first, seg, log_own, gc_own.reshape(shaped)
    )
    gq_other, gk_b, gv_b = attention_backward(
        pieces[1][0], keys, values, second, seg, log_other, gc_other.reshape(shaped)
    )
    flat = (2 * half, 2 * width)
    gk = (gk_a + gk_b).astype(BF).reshape(flat)
    gv = (gv_a + gv_b).astype(BF).reshape(flat)
    gq_own = gq_own.reshape(half, 2 * width)
    gq_other = gq_other.reshape(half, 2 * width)
    gqkv_own = jnp.concatenate([gq_own, gk[:half], gv[:half]], 1)
    gqkv_other = jnp.concatenate([gq_other, gk[half:], gv[half:]], 1)
    got = outer(mm_t(gqkv_other, wqkv).astype(BF))
    grad_wqkv = t_mm(own_in, gqkv_own) + t_mm(other_in, gqkv_other)
    grad_bqkv = jnp.sum(gqkv_own.astype(F32), 0) + jnp.sum(gqkv_other.astype(F32), 0)
    grad_input = mm_t(gqkv_own, wqkv) + got.astype(F32) + grad_one

    by_part = grad_wqkv.reshape(model, 3, 2, width)
    grad_wqkv = pair_sum(
        by_part[:, :, 0].reshape(model, 3 * width), by_part[:, :, 1].reshape(model, 3 * width)
    )
    grad_w_out = pair_sum(grad_w_out[:width], grad_w_out[width:])
    attention_flat = jnp.concatenate([grad_wqkv.astype(BF).reshape(-1, model), grad_w_out.astype(BF)])
    attention_flat = lax.psum(attention_flat, "dp")

    bias_parts = grad_bqkv.reshape(3, 2, width)
    mine = jnp.concatenate([bias_parts[0, 0], bias_parts[2, 0], grad_b_up[:hidden_width]])
    theirs = jnp.concatenate([bias_parts[0, 1], bias_parts[2, 1], grad_b_up[hidden_width:]])
    small = lax.psum(mine + inner(theirs), "dp")
    shared = jnp.stack(
        [grad_b_out, grad_gain_one, grad_shift_one, grad_b_down, grad_gain_two, grad_shift_two]
    )
    shared = lax.psum(shared, ("dp", "tensor"))

    gw_qkv = attention_flat[: 3 * width].reshape(model, 3, width).astype(F32)
    return (
        from_sequence(output),
        from_sequence(grad_input),
        gw_qkv[:, 0],
        gw_qkv[:, 1],
        gw_qkv[:, 2],
        small[:width],
        small[width : 2 * width],
        attention_flat[3 * width :].astype(F32),
        shared[0],
        shared[1],
        shared[2],
        feed_flat[:model].astype(F32),
        small[2 * width :],
        feed_flat[model:].astype(F32),
        shared[3],
        shared[4],
        shared[5],
    )


def solution(mesh):
    tokens = P("dp", "tensor", None)
    columns = P(None, "tensor")
    lines = P("tensor", None)
    split = P("tensor")
    whole = P()
    return jax.shard_map(
        shards,
        mesh=mesh,
        in_specs=(tokens, P("dp", None), tokens, columns, columns, columns, split, split, lines)
        + (whole, whole, whole, columns, split, lines, whole, whole, whole),
        out_specs=(tokens, tokens, columns, columns, columns, split, split, lines, whole, whole, whole)
        + (columns, split, lines, whole, whole, whole),
        check_vma=False,
    )
```

time: 852 us -> 425 us (0.50)
  waiting for transfers between devices: 550 us -> 114 us
  starting transfers between devices: 0.65 us -> 13.8 us
  matrix products: 121 us -> 109 us
  local copies, waits for them, and re-layouts: 35.4 us -> 46.4 us
    reduce_scatter x8 -> x0, waiting for transfers between devices: 231 us -> none  [the longest x2 76 us: micro_pass(): lax.psum_scatter(matmul(context, w_out), 'tensor', scatter_dimension=0, t...]
    all_gather x8 -> x0, waiting for transfers between devices: 144 us -> none  [the longest x2 39.5 us: micro_pass(): lax.all_gather(hidden_one.astype(jnp.bfloat16), 'tensor', axis=0, tiled=T...]
    psum x1, waiting for transfers between devices: 175 us -> 45.4 us  [shards(): attention_flat = lax.psum(attention_flat, 'dp')]
    ppermute x0 -> x23, waiting for transfers between devices: none -> 69.1 us  [the longest x8 67.1 us: outer(): return lax.ppermute(x, 'tensor', [(i, i ^ 2) for i in range(ranks)])]
    reduce_sum x28 -> x9, other arithmetic: 35.4 us -> 13.5 us  [the longest x2 5.56 us: attention_forward(): total = jnp.sum(exponent, -1, keepdims=True)]
    slice x6 -> x25, local copies, waits for them, and re-layouts: 1.67 us -> 22.2 us  [the longest x2 6 us: shards(): gw_qkv[:, 2]]
    convert_element_type x6 -> x10, other arithmetic: 8.77 us -> 28.6 us  [the longest x2 16.1 us: attention_backward(): grad_scores = (weights * (grad_weights - row)).astype(BF)]
    while x256 -> x0, local copies, waits for them, and re-layouts: 18.7 us -> none
  transfers between devices with their start and end apart: 17 -> 24, of which waited for: 17 -> 10; matrix products, arithmetic and copies ran while one was open for 6% -> 40% of each run, Pallas kernels for 0% -> 0%
where the time goes in v1:
time: 425 us; the launch traced here: 418 us
  waiting for transfers between devices  114 us (27%)
  matrix products  109 us (26%)
  blocking collectives  63.9 us (15%)
  other arithmetic  54.8 us (13%)
  local copies, waits for them, and re-layouts  46.4 us (11%)
  between operations  15.6 us (4%)
  starting transfers between devices  13.8 us (3%)
    ppermute x8, waiting for transfers between devices, outer(): return lax.ppermute(x, 'tensor', [(i, i ^ 2) for i in range(ranks)])  67.1 us
    dot_general x24, matrix products, dot(): lax.dot_general(left, right, (contract, ((), ())), preferred_element_type...  63.9 us
    psum x1, waiting for transfers between devices, shards(): attention_flat = lax.psum(attention_flat, 'dp')  45.4 us
    psum x1, blocking collectives, shards(): shared = lax.psum(shared, ('dp', 'tensor'))  42.1 us
    psum x1, blocking collectives, shards(): small = lax.psum(mine + inner(theirs), 'dp')  21.8 us
    convert_element_type x2, other arithmetic, attention_backward(): grad_scores = (weights * (grad_weights - row)).astype(BF)  16.1 us
    dot_general x2, matrix products, attention_backward(): jnp.einsum('qhd,khd->hqk', grad, values, preferred_element_type=F32)  14.7 us
    unnamed x161, local copies, waits for them, and re-layouts  10.7 us
  transfers between devices with their start and end apart: 24, of which 10 were waited for; matrix products, arithmetic and copies ran while one was open for 40% of the time, Pallas kernels for 0%

profile of v1, /device:TPU:0, one launch (start us, length us, event | category | flops | bytes accessed | tf_op | source)
XLA Modules:
  0.0 418.1 jit_solution(3931726033955160622)
XLA Ops:
  15.8 2.6 collective-permute-start.3
  23.5 13.1 %collective-permute-done.3 = bf16[512,768]{1,0:T(8,128)(2,1)} collective-permute-done((bf16[512,768]{1,0:T(8,128)(2,1)S(1)}, bf16[512,768]{1,0:T(8,128)(2,1)}, u32[]{:S(2)}, u32[]{:S(2)}) %collective-permute-start.3) | collective-permute-done | bytes 786464 | tf_op jit(solution)/shard_map/ppermute | solution.py:109
  36.7 2.9 fusion.23
  42.2 3.6 fusion.62
  45.8 2.9 fusion.1
  48.8 2.9 fusion.45
  54.2 2.4 fusion.63
  56.6 2.6 fusion
  59.3 3.5 fusion.46
  62.7 9.0 %collective-permute-done.5 = bf16[512,768]{1,0:T(8,128)(2,1)S(1)} collective-permute-done((bf16[512,768]{1,0:T(8,128)(2,1)S(1)}, bf16[512,768]{1,0:T(8,128)(2,1)S(1)}, u32[]{:S(2)}, u32[]{:S(2)}) %collective-permute-start.5) | collective-permute-done | bytes 786464 | tf_op jit(solution)/shard_map/ppermute | solution.py:109
  81.3 10.5 %collective-permute-done.9 = bf16[512,768]{1,0:T(8,128)(2,1)S(1)} collective-permute-done((bf16[512,768]{1,0:T(8,128)(2,1)S(1)}, bf16[512,768]{1,0:T(8,128)(2,1)S(1)}, u32[]{:S(2)}, u32[]{:S(2)}) %collective-permute-start.9) | collective-permute-done | bytes 786464 | tf_op jit(solution)/shard_map/ppermute | solution.py:109
  97.8 14.9 %collective-permute-done.10 = bf16[512,768]{1,0:T(8,128)(2,1)S(1)} collective-permute-done((bf16[512,768]{1,0:T(8,128)(2,1)S(1)}, bf16[512,768]{1,0:T(8,128)(2,1)S(1)}, u32[]{:S(2)}, u32[]{:S(2)}) %collective-permute-start.10) | collective-permute-done | bytes 786464 | tf_op jit(solution)/shard_map/ppermute | solution.py:109
  116.8 2.8 convert_reduce_fusion.5
  120.5 5.9 %convert_reduce_fusion.1 = (f32[1536]{0:T(1024)}, bf16[512,1536]{1,0:T(8,128)(2,1)}) fusion(f32[512,1536]{1,0:T(8,128)} %copy-done.74, bf16[512,768]{1,0:T(8,128)(2,1)S(1)} %get-tuple-element.52, bf16[1536,768]{1,0:T(8,128)(2,1)S(1)} %constant_dynamic-update-slice_fusion.7), kind=kOutput, calls=%fused_computation.46 | convolution fusion | flops 1224473088 | bytes 7870464 | tf_op jit(solution)/shard_map/dot_general | solution.py:15
  126.4 3.0 fusion.68
  129.4 3.9 fusion.51
  133.3 3.1 collective-permute-done.13
  136.4 5.3 %convert_reduce_fusion = (f32[1536]{0:T(1024)}, bf16[512,1536]{1,0:T(8,128)(2,1)S(1)}) fusion(f32[512,1536]{1,0:T(8,128)S(1)} %convolution_add_fusion.5, bf16[512,768]{1,0:T(8,128)(2,1)} %collective-permute-done.13, bf16[1536,768]{1,0:T(8,128)(2,1)} %copy-done.53), kind=kOutput, calls=%fused_computation.45 | convolution fusion | flops 1224473088 | bytes 7870464 | tf_op jit(solution)/shard_map/dot_general | solution.py:15
  141.7 4.6 %convolution_convert_fusion = bf16[512,768]{1,0:T(8,128)(2,1)} fusion(bf16[512,1536]{1,0:T(8,128)(2,1)S(1)} %get-tuple-element.109, bf16[768,1536]{1,0:T(8,128)(2,1)} %copy-done.54), kind=kOutput, calls=%fused_computation.95 | convolution fusion | flops 1208352768 | bytes 4718592 | tf_op jit(solution)/shard_map/dot_general | solution.py:15
  146.9 5.4 %convolution_add_fusion.1 = f32[1536,768]{1,0:T(8,128)S(1)} fusion(f32[1536,768]{1,0:T(8,128)} %fusion.51, bf16[512,768]{1,0:T(8,128)(2,1)} %collective-permute-done.13, f32[512,1536]{1,0:T(8,128)} %copy-done.5), kind=kOutput, calls=%fused_computation.27 | convolution fusion | flops 1216217088 | bytes 13369344 | tf_op jit(solution)/shard_map/dot_general | solution.py:15
  155.7 3.7 convolution_add_fusion.2
  159.4 2.8 slice.342
  162.5 4.8 %multiply_reduce_fusion.2 = (f32[768]{0:T(1024)}, f32[512]{0:T(512)S(1)}, f32[512]{0:T(512)S(1)}, f32[768]{0:T(1024)}, f32[512,768]{1,0:T(8,128)S(1)}) fusion(f32[512,768]{1,0:T(8,128)S(1)} %get-tuple-element.98, f32[512]{0:T(512)S(1)} %add_rsqrt_fusion.1, f32[512]{0:T(512)S(1)} %broadcast_multiply_fusion.5, f32[768]{0:T(1024)S(1)} %copy-done.60, ...), kind=kOutput, calls=%fused_computation.78 | convolution fusion | flops 1219360256 | bytes 10252289 | tf_op jit(solution)/shard_map/dot_general | solution.py:15
  167.3 2.7 convert_reduce_fusion.6
  170.0 2.4 convolution_convert_fusion.5
  173.6 7.5 %multiply_reduce_fusion.1 = (f32[6,512]{1,0:T(8,128)}, f32[6,512,1024]{2,1,0:T(8,128)}) fusion(f32[6,512,1024]{2,1,0:T(8,128)S(1)} %get-tuple-element.96, f32[6,512]{1,0:T(8,128)S(1)} %log_add_fusion.1, bf16[512,6,64]{0,2,1:T(8,128)(2,1)} %bitcast.173, bf16[512,6,64]{0,2,1:T(8,128)(2,1)S(1)} %bitcast.149, bf16[512,6,64]{0,2,1:T(8,128)(2,1)S(1)} %bitcast.144), kind=kOutput, calls=%fused_computation.4 | convolution fusion | flops 413660160 | bytes 26370048 | tf_op jit(solution)/shard_map/qhd,khd->hqk/dot_general | solution.py:67
  181.1 9.2 %multiply_convert_fusion.1 = bf16[6,512,1024]{2,1,0:T(8,128)(2,1)} fusion(f32[6,512,1024]{2,1,0:T(8,128)} %get-tuple-element.103, f32[6,512,1024]{2,1,0:T(8,128)S(1)} %get-tuple-element.96, f32[6,512]{1,0:T(8,128)} %get-tuple-element.102, f32[6,512]{1,0:T(8,128)S(1)} %log_add_fusion.1), kind=kLoop, calls=%fused_computation.3 | loop fusion | flops 12582912 | bytes 31481856 | tf_op jit(solution)/shard_map/convert_element_type | solution.py:69
  190.4 5.7 %fusion.43 = bf16[6,64,512]{2,1,0:T(8,128)(2,1)} fusion(bf16[6,512,1024]{2,1,0:T(8,128)(2,1)} %multiply_convert_fusion.1, bf16[512,6,64]{0,2,1:T(8,128)(2,1)S(1)} %bitcast.140, bf16[512,6,64]{0,2,1:T(8,128)(2,1)S(1)} %bitcast.136), kind=kOutput, calls=%fused_computation.105 | convolution fusion | flops 404619264 | bytes 7471104 | tf_op jit(solution)/shard_map/hqk,khd->qhd/dot_general | solution.py:70
  196.1 2.8 fusion.67
  201.2 2.7 fusion.26
  206.2 3.2 fusion.4
  209.4 7.2 %multiply_reduce_fusion = (f32[6,512]{1,0:T(8,128)S(1)}, f32[6,512,1024]{2,1,0:T(8,128)}) fusion(f32[6,512,1024]{2,1,0:T(8,128)S(1)} %get-tuple-element.94, f32[6,512]{1,0:T(8,128)S(1)} %log_add_fusion, bf16[512,6,64]{0,2,1:T(8,128)(2,1)} %bitcast.176, bf16[512,6,64]{0,2,1:T(8,128)(2,1)} %bitcast.147, bf16[512,6,64]{0,2,1:T(8,128)(2,1)S(1)} %bitcast.145), kind=kOutput, calls=%fused_computation.1 | convolution fusion | flops 413660160 | bytes 26370048 | tf_op jit(solution)/shard_map/qhd,khd->hqk/dot_general | solution.py:67
  216.6 3.6 fusion.39
  220.4 6.9 %multiply_convert_fusion = bf16[6,512,1024]{2,1,0:T(8,128)(2,1)S(1)} fusion(f32[6,512,1024]{2,1,0:T(8,128)} %get-tuple-element.105, f32[6,512,1024]{2,1,0:T(8,128)S(1)} %get-tuple-element.94, f32[6,512]{1,0:T(8,128)S(1)} %get-tuple-element.104, f32[6,512]{1,0:T(8,128)S(1)} %log_add_fusion), kind=kLoop, calls=%fused_computation | loop fusion | flops 12582912 | bytes 31481856 | tf_op jit(solution)/shard_map/convert_element_type | solution.py:69
  230.7 2.5 fusion.50
  234.5 3.0 copy.63
  239.4 2.4 fusion.27
  256.5 16.2 %collective-permute-done.16 = bf16[512,768]{1,0:T(8,128)(2,1)S(1)} collective-permute-done((bf16[512,768]{1,0:T(8,128)(2,1)S(1)}, bf16[512,768]{1,0:T(8,128)(2,1)S(1)}, u32[]{:S(2)}, u32[]{:S(2)}) %collective-permute-start.16) | collective-permute-done | bytes 786464 | tf_op jit(solution)/shard_map/ppermute | solution.py:109
  275.1 42.1 %psum.30 = f32[6,768]{1,0:T(8,128)S(1)} all-reduce(f32[6,768]{1,0:T(8,128)S(1)} %stack.75), channel_id=1, replica_groups=mesh['dp'=8,'tensor'=4] {'dp','tensor'}, use_global_device_ids=true, to_apply=%region_26.27 | all-reduce | flops 4608 | bytes 36864 | tf_op jit(solution)/shard_map/psum | solution.py:239
  319.1 21.8 %psum.29 = f32[1152]{0:T(1024)S(1)} all-reduce(f32[1152]{0:T(1024)S(1)} %add.245), channel_id=1, replica_groups=mesh['dp'=8,'tensor'=4] {'dp'}, use_global_device_ids=true, to_apply=%region_19.20 | all-reduce | flops 1152 | bytes 9216 | tf_op jit(solution)/shard_map/psum | solution.py:235
  342.2 2.7 maximum_select_fusion
  344.8 45.4 %all-reduce.3.cloned.1.call-done = (bf16[768,768]{1,0:T(8,128)(2,1)}, bf16[1536,768]{1,0:T(8,128)(2,1)}) async-done(((bf16[768,768]{1,0:T(8,128)(2,1)}, bf16[1536,768]{1,0:T(8,128)(2,1)}), (bf16[768,768]{1,0:T(8,128)(2,1)}, bf16[1536,768]{1,0:T(8,128)(2,1)})) %all-reduce.3.cloned.1.call-update) | async-done | bytes 3538960 | tf_op jit(solution)/shard_map/psum | solution.py:230
  392.0 2.5 slice_convert_fusion.5
  394.5 3.5 reshape.255
  398.0 2.9 fusion.54
  401.0 3.1 copy.67
  404.0 2.9 copy.66
  408.6 2.5 slice_convert_fusion.3
  (296 shorter events, 78.8 us)
Async XLA Ops:
  7.2 383.0 %all-reduce.3.cloned.1.call-start = ((), (), s32[]{:S(2)}) async-start(), calls=%async_computation | async-start | bytes 7077888 | tf_op jit(solution)/shard_map/psum | solution.py:230
  8.0 6.6 %collective-permute-start.2 = (f32[1,2,192]{2,1,0:T(2,128)S(1)}, f32[1,2,192]{2,1,0:T(2,128)S(1)}, u32[]{:S(2)}, u32[]{:S(2)}) collective-permute-start(f32[1,2,192]{2,1,0:T(2,128)S(1)} %maximum_bitcast_fusion.1), channel_id=1, source_target_pairs={{0,1},{1,0},{2,3},{3,2},{4,5},{5,4},{6,7},{7,6},{8,9},{9,8},{10,11... | collective-permute-start | bytes 4616 | tf_op jit(solution)/shard_map/ppermute | solution.py:106
  8.6 69.0 %collective-permute-start.7 = (f32[768]{0:T(1024)}, f32[768]{0:T(1024)S(1)}, u32[]{:S(2)}, u32[]{:S(2)}) collective-permute-start(f32[768]{0:T(1024)} %param.31), channel_id=1, source_target_pairs={{0,1},{1,0},{2,3},{3,2},{4,5},{5,4},{6,7},{7,6},{8,9},{9,8},{10,11... | collective-permute-start | bytes 9224 | tf_op jit(solution)/shard_map/ppermute | solution.py:106
  8.6 7.1 %collective-permute-start.4 = (bf16[192,768]{1,0:T(8,128)(2,1)}, bf16[192,768]{1,0:T(8,128)(2,1)}, u32[]{:S(2)}, u32[]{:S(2)}) collective-permute-start(bf16[192,768]{1,0:T(8,128)(2,1)} %param.26), channel_id=1, source_target_pairs={{0,1},{1,0},{2,3},{3,2},{4,5},{5,4},{6,7},{7,6},{8,9},{9,8},{10,11... | collective-permute-start | bytes 884744 | tf_op jit(solution)/shard_map/ppermute | solution.py:106
  10.3 4.7 %collective-permute-start = (bf16[256,768]{1,0:T(8,128)(2,1)S(1)}, bf16[256,768]{1,0:T(8,128)(2,1)S(1)}, u32[]{:S(2)}, u32[]{:S(2)}) collective-permute-start(bf16[256,768]{1,0:T(8,128)(2,1)S(1)} %get-tuple-element.80), channel_id=1, source_target_pairs={{0,1},{1,0},{2,3},{3,2},{4,5},{5,4},{6,7},{7,6},{8,9},{9,8},{10,11... | collective-permute-start | bytes 1179656 | tf_op jit(solution)/shard_map/ppermute | solution.py:106
  11.5 7.9 %collective-permute-start.1 = (bf16[1,768,576]{1,2,0:T(8,128)(2,1)S(1)}, bf16[1,768,576]{1,2,0:T(8,128)(2,1)}, u32[]{:S(2)}, u32[]{:S(2)}) collective-permute-start(bf16[1,768,576]{1,2,0:T(8,128)(2,1)S(1)} %bitcast.161), channel_id=1, source_target_pairs={{0,1},{1,0},{2,3},{3,2},{4,5},{5,4},{6,7},{7,6},{8,9},{9,8},{10,11... | collective-permute-start | bytes 2654216 | tf_op jit(solution)/shard_map/ppermute | solution.py:106
  14.6 63.0 %collective-permute-start.6 = (bf16[768,768]{1,0:T(8,128)(2,1)}, bf16[768,768]{1,0:T(8,128)(2,1)}, u32[]{:S(2)}, u32[]{:S(2)}) collective-permute-start(bf16[768,768]{1,0:T(8,128)(2,1)} %param.30), channel_id=1, source_target_pairs={{0,1},{1,0},{2,3},{3,2},{4,5},{5,4},{6,7},{7,6},{8,9},{9,8},{10,11... | collective-permute-start | bytes 3538952 | tf_op jit(solution)/shard_map/ppermute | solution.py:106
  15.0 64.1 %collective-permute-start.8 = (bf16[768,768]{1,0:T(8,128)(2,1)}, bf16[768,768]{1,0:T(8,128)(2,1)}, u32[]{:S(2)}, u32[]{:S(2)}) collective-permute-start(bf16[768,768]{1,0:T(8,128)(2,1)} %param.32), channel_id=1, source_target_pairs={{0,1},{1,0},{2,3},{3,2},{4,5},{5,4},{6,7},{7,6},{8,9},{9,8},{10,11... | collective-permute-start | bytes 3538952 | tf_op jit(solution)/shard_map/ppermute | solution.py:106
  15.8 55.9 %copy-start.3 = (bf16[512,768]{1,0:T(8,128)(2,1)}, bf16[512,768]{1,0:T(8,128)(2,1)S(1)}, u32[]{:S(2)}) copy-start(bf16[512,768]{1,0:T(8,128)(2,1)S(1)} %maximum_select_fusion.1) | copy-start | bytes 2359300
  15.8 20.9 %collective-permute-start.3 = (bf16[512,768]{1,0:T(8,128)(2,1)S(1)}, bf16[512,768]{1,0:T(8,128)(2,1)}, u32[]{:S(2)}, u32[]{:S(2)}) collective-permute-start(bf16[512,768]{1,0:T(8,128)(2,1)S(1)} %maximum_select_fusion.1), channel_id=1, source_target_pairs={{0,2},{1,3},{2,0},{3,1},{4,6},{5,7},{6,4},{7,5},{8,10},{9,11},{10,... | collective-permute-start | bytes 2359304 | tf_op jit(solution)/shard_map/ppermute | solution.py:109
  23.3 167.0 %copy-start.14 = (bf16[512,384]{0,1:T(8,128)(2,1)}, bf16[512,384]{0,1:T(8,128)(2,1)S(1)}, u32[]{:S(2)}) copy-start(bf16[512,384]{0,1:T(8,128)(2,1)S(1)} %copy.60) | copy-start | bytes 1179652
  23.5 25.2 %copy-start.18 = (bf16[512,384]{0,1:T(8,128)(2,1)}, bf16[512,384]{0,1:T(8,128)(2,1)S(1)}, u32[]{:S(2)}) copy-start(bf16[512,384]{0,1:T(8,128)(2,1)S(1)} %copy.57) | copy-start | bytes 1179652
  40.7 8.1 %copy-start.22 = (bf16[512,384]{0,1:T(8,128)(2,1)}, bf16[512,384]{0,1:T(8,128)(2,1)S(1)}, u32[]{:S(2)}) copy-start(bf16[512,384]{0,1:T(8,128)(2,1)S(1)} %copy.58) | copy-start | bytes 1179652
  42.2 148.1 %copy-start.16 = (bf16[512,384]{0,1:T(8,128)(2,1)}, bf16[512,384]{0,1:T(8,128)(2,1)S(1)}, u32[]{:S(2)}) copy-start(bf16[512,384]{0,1:T(8,128)(2,1)S(1)} %copy.61) | copy-start | bytes 1179652
  52.3 19.4 %collective-permute-start.5 = (bf16[512,768]{1,0:T(8,128)(2,1)S(1)}, bf16[512,768]{1,0:T(8,128)(2,1)S(1)}, u32[]{:S(2)}, u32[]{:S(2)}) collective-permute-start(bf16[512,768]{1,0:T(8,128)(2,1)S(1)} %convolution_convert_fusion.3), channel_id=1, source_target_pairs={{0,2},{1,3},{2,0},{3,1},{4,6},{5,7},{6,4},{7,5},{8,10},{9,11},{10,... | collective-permute-start | bytes 2359304 | tf_op jit(solution)/shard_map/ppermute | solution.py:109
  59.2 12.5 %copy-start.71 = (f32[768]{0:T(1024)S(1)}, f32[768]{0:T(1024)}, u32[]{:S(2)}) copy-start(f32[768]{0:T(1024)} %param.27) | copy-start | bytes 9220
  62.7 10.1 %copy-start.40 = (bf16[6,64,512]{2,1,0:T(8,128)(2,1)}, bf16[6,64,512]{2,1,0:T(8,128)(2,1)S(1)}, u32[]{:S(2)}) copy-start(bf16[6,64,512]{2,1,0:T(8,128)(2,1)S(1)} %fusion.46) | copy-start | bytes 1179652
  73.2 18.5 %collective-permute-start.9 = (bf16[512,768]{1,0:T(8,128)(2,1)S(1)}, bf16[512,768]{1,0:T(8,128)(2,1)S(1)}, u32[]{:S(2)}, u32[]{:S(2)}) collective-permute-start(bf16[512,768]{1,0:T(8,128)(2,1)S(1)} %fusion.38), channel_id=1, source_target_pairs={{0,2},{1,3},{2,0},{3,1},{4,6},{5,7},{6,4},{7,5},{8,10},{9,11},{10,... | collective-permute-start | bytes 2359304 | tf_op jit(solution)/shard_map/ppermute | solution.py:109
  74.8 40.6 %collective-permute-start.12 = (bf16[256,768]{1,0:T(8,128)(2,1)S(1)}, bf16[256,768]{1,0:T(8,128)(2,1)S(1)}, u32[]{:S(2)}, u32[]{:S(2)}) collective-permute-start(bf16[256,768]{1,0:T(8,128)(2,1)S(1)} %get-tuple-element.75), channel_id=1, source_target_pairs={{0,1},{1,0},{2,3},{3,2},{4,5},{5,4},{6,7},{7,6},{8,9},{9,8},{10,11... | collective-permute-start | bytes 1179656 | tf_op jit(solution)/shard_map/ppermute | solution.py:106
  79.0 17.4 %copy-start.54 = (bf16[768,1536]{1,0:T(8,128)(2,1)}, bf16[768,1536]{1,0:T(8,128)(2,1)S(1)}, u32[]{:S(2)}) copy-start(bf16[768,1536]{1,0:T(8,128)(2,1)S(1)} %constant_dynamic-update-slice_fusion.5) | copy-start | bytes 7077892
  81.2 39.2 %copy-start.53 = (bf16[1536,768]{1,0:T(8,128)(2,1)}, bf16[1536,768]{1,0:T(8,128)(2,1)S(1)}, u32[]{:S(2)}) copy-start(bf16[1536,768]{1,0:T(8,128)(2,1)S(1)} %constant_dynamic-update-slice_fusion.7) | copy-start | bytes 7077892
  93.1 43.3 %copy-start.5 = (f32[512,1536]{1,0:T(8,128)}, f32[512,1536]{1,0:T(8,128)S(1)}, u32[]{:S(2)}) copy-start(f32[512,1536]{1,0:T(8,128)S(1)} %convolution_add_fusion.5) | copy-start | bytes 9437188
  95.1 17.7 %collective-permute-start.10 = (bf16[512,768]{1,0:T(8,128)(2,1)S(1)}, bf16[512,768]{1,0:T(8,128)(2,1)S(1)}, u32[]{:S(2)}, u32[]{:S(2)}) collective-permute-start(bf16[512,768]{1,0:T(8,128)(2,1)S(1)} %convolution_convert_fusion.1), channel_id=1, source_target_pairs={{0,2},{1,3},{2,0},{3,1},{4,6},{5,7},{6,4},{7,5},{8,10},{9,11},{10,... | collective-permute-start | bytes 2359304 | tf_op jit(solution)/shard_map/ppermute | solution.py:109
  96.4 16.4 %copy-start.73 = (f32[768]{0:T(1024)S(1)}, f32[768]{0:T(1024)}, u32[]{:S(2)}) copy-start(f32[768]{0:T(1024)} %param.33) | copy-start | bytes 9220
  97.8 17.3 %copy-start.74 = (f32[512,1536]{1,0:T(8,128)}, f32[512,1536]{1,0:T(8,128)S(1)}, u32[]{:S(2)}) copy-start(f32[512,1536]{1,0:T(8,128)S(1)} %convolution_add_fusion.6) | copy-start | bytes 9437188
  97.8 17.6 %copy-start.59 = (f32[768]{0:T(1024)S(1)}, f32[768]{0:T(1024)}, u32[]{:S(2)}) copy-start(f32[768]{0:T(1024)} %param.34) | copy-start | bytes 9220
  119.6 16.8 %collective-permute-start.13 = (bf16[512,768]{1,0:T(8,128)(2,1)S(1)}, bf16[512,768]{1,0:T(8,128)(2,1)}, u32[]{:S(2)}, u32[]{:S(2)}) collective-permute-start(bf16[512,768]{1,0:T(8,128)(2,1)S(1)} %get-tuple-element.52), channel_id=1, source_target_pairs={{0,2},{1,3},{2,0},{3,1},{4,6},{5,7},{6,4},{7,5},{8,10},{9,11},{10,... | collective-permute-start | bytes 2359304 | tf_op jit(solution)/shard_map/ppermute | solution.py:109
  146.3 16.2 %collective-permute-start.14 = (bf16[512,768]{1,0:T(8,128)(2,1)}, bf16[512,768]{1,0:T(8,128)(2,1)}, u32[]{:S(2)}, u32[]{:S(2)}) collective-permute-start(bf16[512,768]{1,0:T(8,128)(2,1)} %convolution_convert_fusion), channel_id=1, source_target_pairs={{0,2},{1,3},{2,0},{3,1},{4,6},{5,7},{6,4},{7,5},{8,10},{9,11},{10,... | collective-permute-start | bytes 2359304 | tf_op jit(solution)/shard_map/ppermute | solution.py:109
  153.5 9.0 %copy-start.35 = (bf16[512,1536]{1,0:T(8,128)(2,1)S(1)}, bf16[512,1536]{1,0:T(8,128)(2,1)}, u32[]{:S(2)}) copy-start(bf16[512,1536]{1,0:T(8,128)(2,1)} %get-tuple-element.107) | copy-start | bytes 4718596
  153.5 47.6 %collective-permute-start.22 = (bf16[768,768]{1,0:T(8,128)(2,1)}, bf16[768,768]{1,0:T(8,128)(2,1)}, u32[]{:S(2)}, u32[]{:S(2)}) collective-permute-start(bf16[768,768]{1,0:T(8,128)(2,1)} %slice.341), channel_id=1, source_target_pairs={{0,1},{1,0},{2,3},{3,2},{4,5},{5,4},{6,7},{7,6},{8,9},{9,8},{10,11... | collective-permute-start | bytes 3538952 | tf_op jit(solution)/shard_map/ppermute | solution.py:106
  162.3 77.1 %collective-permute-start.21 = (bf16[768,768]{1,0:T(8,128)(2,1)}, bf16[768,768]{1,0:T(8,128)(2,1)}, u32[]{:S(2)}, u32[]{:S(2)}) collective-permute-start(bf16[768,768]{1,0:T(8,128)(2,1)} %slice.342), channel_id=1, source_target_pairs={{0,1},{1,0},{2,3},{3,2},{4,5},{5,4},{6,7},{7,6},{8,9},{9,8},{10,11... | collective-permute-start | bytes 3538952 | tf_op jit(solution)/shard_map/ppermute | solution.py:106
  172.4 31.4 %collective-permute-start.15 = (bf16[512,768]{1,0:T(8,128)(2,1)}, bf16[512,768]{1,0:T(8,128)(2,1)}, u32[]{:S(2)}, u32[]{:S(2)}) collective-permute-start(bf16[512,768]{1,0:T(8,128)(2,1)} %get-tuple-element.54), channel_id=1, source_target_pairs={{0,2},{1,3},{2,0},{3,1},{4,6},{5,7},{6,4},{7,5},{8,10},{9,11},{10,... | collective-permute-start | bytes 2359304 | tf_op jit(solution)/shard_map/ppermute | solution.py:109
  190.4 8.5 %copy-start = (bf16[6,512,1024]{2,1,0:T(8,128)(2,1)S(1)}, bf16[6,512,1024]{2,1,0:T(8,128)(2,1)}, u32[]{:S(2)}) copy-start(bf16[6,512,1024]{2,1,0:T(8,128)(2,1)} %multiply_convert_fusion.1) | copy-start | bytes 18874372
  220.4 10.3 %copy-start.43 = (bf16[512,6,64]{0,2,1:T(8,128)(2,1)}, bf16[512,6,64]{0,2,1:T(8,128)(2,1)S(1)}, u32[]{:S(2)}) copy-start(bf16[512,6,64]{0,2,1:T(8,128)(2,1)S(1)} %get-tuple-element.74) | copy-start | bytes 1179652
  220.4 12.9 %copy-start.10 = (bf16[512,6,64]{0,2,1:T(8,128)(2,1)}, bf16[512,6,64]{0,2,1:T(8,128)(2,1)S(1)}, u32[]{:S(2)}) copy-start(bf16[512,6,64]{0,2,1:T(8,128)(2,1)S(1)} %get-tuple-element.73) | copy-start | bytes 1179652
  239.1 7.5 %collective-permute-start.18 = (bf16[768,576]{0,1:T(8,128)(2,1)S(1)}, bf16[768,576]{0,1:T(8,128)(2,1)S(1)}, u32[]{:S(2)}, u32[]{:S(2)}) collective-permute-start(bf16[768,576]{0,1:T(8,128)(2,1)S(1)} %bitcast.177), channel_id=1, source_target_pairs={{0,1},{1,0},{2,3},{3,2},{4,5},{5,4},{6,7},{7,6},{8,9},{9,8},{10,11... | collective-permute-start | bytes 2654216 | tf_op jit(solution)/shard_map/ppermute | solution.py:106
  243.6 3.0 collective-permute-start.19
  252.9 19.8 %copy-start.9 = (bf16[6,64,512]{2,1,0:T(8,128)(2,1)S(1)}, bf16[6,64,512]{2,1,0:T(8,128)(2,1)}, u32[]{:S(2)}) copy-start(bf16[6,64,512]{2,1,0:T(8,128)(2,1)} %fusion.43) | copy-start | bytes 1179652
  252.9 19.8 %copy-start.11 = (bf16[512,6,64]{0,2,1:T(8,128)(2,1)S(1)}, bf16[512,6,64]{0,2,1:T(8,128)(2,1)}, u32[]{:S(2)}) copy-start(bf16[512,6,64]{0,2,1:T(8,128)(2,1)} %copy-done.10) | copy-start | bytes 1179652
  253.0 19.8 %copy-start.13 = (bf16[512,6,64]{0,2,1:T(8,128)(2,1)S(1)}, bf16[512,6,64]{0,2,1:T(8,128)(2,1)}, u32[]{:S(2)}) copy-start(bf16[512,6,64]{0,2,1:T(8,128)(2,1)} %copy-done.12) | copy-start | bytes 1179652
  253.0 19.8 %copy-start.42 = (f32[512,768]{1,0:T(8,128)S(1)}, f32[512,768]{1,0:T(8,128)}, u32[]{:S(2)}) copy-start(f32[512,768]{1,0:T(8,128)} %get-tuple-element.55) | copy-start | bytes 4718596
  253.0 19.7 %collective-permute-start.16 = (bf16[512,768]{1,0:T(8,128)(2,1)S(1)}, bf16[512,768]{1,0:T(8,128)(2,1)S(1)}, u32[]{:S(2)}, u32[]{:S(2)}) collective-permute-start(bf16[512,768]{1,0:T(8,128)(2,1)S(1)} %convolution_convert_fusion.2), channel_id=1, source_target_pairs={{0,2},{1,3},{2,0},{3,1},{4,6},{5,7},{6,4},{7,5},{8,10},{9,11},{10,... | collective-permute-start | bytes 2359304 | tf_op jit(solution)/shard_map/ppermute | solution.py:109
  253.7 1.8 collective-permute-start.11
  274.0 43.2 %copy-start.45 = (bf16[512,6,64]{0,2,1:T(8,128)(2,1)S(1)}, bf16[512,6,64]{0,2,1:T(8,128)(2,1)}, u32[]{:S(2)}) copy-start(bf16[512,6,64]{0,2,1:T(8,128)(2,1)} %copy-done.43) | copy-start | bytes 1179652
  274.0 43.2 %copy-start.48 = (bf16[512,6,64]{0,2,1:T(8,128)(2,1)S(1)}, bf16[512,6,64]{0,2,1:T(8,128)(2,1)}, u32[]{:S(2)}) copy-start(bf16[512,6,64]{0,2,1:T(8,128)(2,1)} %copy-done.46) | copy-start | bytes 1179652
  275.0 67.1 %collective-permute-start.17 = (f32[256,768]{1,0:T(8,128)}, f32[256,768]{1,0:T(8,128)}, u32[]{:S(2)}, u32[]{:S(2)}) collective-permute-start(f32[256,768]{1,0:T(8,128)} %get-tuple-element.63), channel_id=1, source_target_pairs={{0,1},{1,0},{2,3},{3,2},{4,5},{5,4},{6,7},{7,6},{8,9},{9,8},{10,11... | collective-permute-start | bytes 2359304 | tf_op jit(solution)/shard_map/ppermute | solution.py:106
  317.9 1.2 collective-permute-start.20
  401.0 7.6 %copy-start.27 = (bf16[1536,768]{1,0:T(8,128)(2,1)S(1)}, bf16[1536,768]{1,0:T(8,128)(2,1)}, u32[]{:S(2)}) copy-start(bf16[1536,768]{1,0:T(8,128)(2,1)} %get-tuple-element.50) | copy-start | bytes 7077892
  (54 other events, 164.2 us)
Sparse Core Ops, SparseCore 0:
  250.1 140.0 all-reduce.2
